TPU v7x, 256 devices: a whole 4x4x8 slice. The times are simulated.
256 devices in a mesh: replica: 4 (over z_hi, core), fsdp: 64 (over z_lo, x, y).
Axes of the slice: x: 4, y: 4, z: 8 (z_hi: 2, z_lo: 4; z = z_hi * 4 + z_lo), core: 2. Of those that a mesh axis runs over, the one named last changes fastest.
Arguments:
- tokens: bfloat16 [65536, 2048], P(('replica', 'fsdp')), may hold values from -6 to 6
- inner_q: bfloat16 [4, 2048, 2048], P('replica', 'fsdp')
- inner_k: bfloat16 [4, 2048, 512], P('replica', 'fsdp')
- inner_v: bfloat16 [4, 2048, 512], P('replica', 'fsdp')
- outer_q: float32 [2048, 2048], P('fsdp')
- outer_k: float32 [2048, 512], P('fsdp')
- outer_v: float32 [2048, 512], P('fsdp')
- moment_q: float32 [2048, 2048], P('fsdp', 'replica'), may hold values from -0.09375 to 0.09375
- moment_k: float32 [2048, 512], P('fsdp', 'replica'), may hold values from -0.09375 to 0.09375
- value_momentum: float32 [2048, 512], P('fsdp', 'replica'), may hold values from -0.09375 to 0.09375
Outputs:
- projected: bfloat16 [65536, 3072], P(('replica', 'fsdp'))
- updated_outer_query: float32 [2048, 2048], P('fsdp')
- updated_outer_key: float32 [2048, 512], P('fsdp')
- new_outer_v: float32 [2048, 512], P('fsdp')
- new_moment_q: float32 [2048, 2048], P('fsdp', 'replica')
- new_moment_k: float32 [2048, 512], P('fsdp', 'replica')
- new_moment_v: float32 [2048, 512], P('fsdp', 'replica')
All inputs are finite; a program needn't handle non-finite values.
Results may differ from a plain program's by a relative error of at most 0.005.
Values may be sent and summed in bfloat16 or wider, within the bound.
A program may use at most 64 MiB of HBM per device.

v0:
```python
import jax
import jax.numpy as jnp
from jax import lax
from jax.sharding import PartitionSpec as P

LEARN_RATE = 0.7
MOMENTUM_BETA = 0.9


def per_device(
    tokens, inner_q, inner_k, inner_v, outer_q, outer_k, outer_v, moment_q, moment_k, value_momentum
):
    worker_count = lax.axis_size("replica")
    worker_index = lax.axis_index("replica")
    outers = (outer_q, outer_k, outer_v)
    moments = (moment_q, moment_k, value_momentum)
    differences = tuple(
        (
            outer - inner[0].astype(jnp.float32)
            for outer, inner in zip(outers, (inner_q, inner_k, inner_v))
        )
    )
    summed = lax.psum_scatter(differences, "replica", scatter_dimension=1, tiled=True)
    owned_outer = []
    owned_moment = []
    for total, outer, outer_momentum in zip(summed, outers, moments):
        width = outer_momentum.shape[1]
        pseudo = total / worker_count
        new_moment = MOMENTUM_BETA * outer_momentum + pseudo
        own_slice = lax.dynamic_slice_in_dim(outer, worker_index * width, width, 1)
        owned_outer.append(own_slice - LEARN_RATE * (pseudo + MOMENTUM_BETA * new_moment))
        owned_moment.append(new_moment)
    full_outer = lax.all_gather(tuple(owned_outer), "replica", axis=1, tiled=True)
    local_fresh = jnp.concatenate([weight.astype(jnp.bfloat16) for weight in full_outer], axis=1)
    fresh = lax.all_gather(local_fresh, "fsdp", axis=0, tiled=True)
    projected = jnp.dot(tokens, fresh, preferred_element_type=jnp.float32).astype(jnp.bfloat16)
    return (
        projected,
        full_outer[0],
        full_outer[1],
        full_outer[2],
        owned_moment[0],
        owned_moment[1],
        owned_moment[2],
    )


def solution(mesh):
    placed = (
        P(("replica", "fsdp"), None),
        P("replica", "fsdp", None),
        P("replica", "fsdp", None),
        P("replica", "fsdp", None),
        P("fsdp", None),
        P("fsdp", None),
        P("fsdp", None),
        P("fsdp", "replica"),
        P("fsdp", "replica"),
        P("fsdp", "replica"),
    )
    return jax.shard_map(
        per_device,
        mesh=mesh,
        in_specs=placed,
        out_specs=(
            P(("replica", "fsdp"), None),
            P("fsdp", None),
            P("fsdp", None),
            P("fsdp", None),
            P("fsdp", "replica"),
            P("fsdp", "replica"),
            P("fsdp", "replica"),
        ),
        check_vma=False,
    )
```

profile of v0, /device:TPU:16, one launch (start us, length us, event | category | flops | bytes accessed | tf_op | source)
XLA Modules:
  0.0 515.0 jit_solution(6536881610488813657)
XLA Ops:
  7.2 0.0 copy-start
  7.2 0.0 reduce-scatter.6.cloned.1.call-start
  7.2 1.6 convert_subtract_fusion.2
  8.8 0.0 reduce-scatter.6.cloned.1.call-update
  8.8 0.0 reduce-scatter.8.cloned.1.call-start
  8.9 1.5 convert_subtract_fusion.1
  10.3 0.0 reduce-scatter.8.cloned.1.call-update
  10.4 0.0 reduce-scatter.4.cloned.1.call-start
  10.4 1.7 convert_subtract_fusion
  12.1 0.0 reduce-scatter.4.cloned.1.call-update
  12.2 0.0 all-gather.2.cloned.1.call-start
  12.2 36.2 %reduce-scatter.6.cloned.1.call-done = f32[32,128]{1,0:T(8,128)} async-done(((f32[32,512]{1,0:T(8,128)}), f32[32,128]{1,0:T(8,128)}) %reduce-scatter.6.cloned.1.call-update) | async-done | bytes 16400 | tf_op jit(solution)/shard_map/reduce_scatter | solution.py:23
  48.4 1.4 multiply_subtract_fusion.2
  49.8 9.1 %all_gather.13 = f32[32,512]{1,0:T(8,128)S(1)} all-gather(f32[32,128]{1,0:T(8,128)S(1)} %get-tuple-element.16), channel_id=1, replica_groups=mesh['replica'=4,'fsdp'=64] {'replica'}, dimensions={1}, use_global_device_ids=true | all-gather | bytes 81920 | tf_op jit(solution)/shard_map/all_gather | solution.py:33
  58.9 23.6 %reduce-scatter.8.cloned.1.call-done = f32[32,128]{1,0:T(8,128)} async-done(((f32[32,512]{1,0:T(8,128)}), f32[32,128]{1,0:T(8,128)}) %reduce-scatter.8.cloned.1.call-update) | async-done | bytes 16400 | tf_op jit(solution)/shard_map/reduce_scatter | solution.py:23
  82.5 1.4 multiply_subtract_fusion.1
  83.9 9.1 %all_gather.14 = f32[32,512]{1,0:T(8,128)S(1)} all-gather(f32[32,128]{1,0:T(8,128)S(1)} %get-tuple-element.18), channel_id=1, replica_groups=mesh['replica'=4,'fsdp'=64] {'replica'}, dimensions={1}, use_global_device_ids=true | all-gather | bytes 81920 | tf_op jit(solution)/shard_map/all_gather | solution.py:33
  93.0 25.5 %reduce-scatter.4.cloned.1.call-done = f32[32,512]{1,0:T(8,128)} async-done(((f32[32,2048]{1,0:T(8,128)}), f32[32,512]{1,0:T(8,128)}) %reduce-scatter.4.cloned.1.call-update) | async-done | bytes 65552 | tf_op jit(solution)/shard_map/reduce_scatter | solution.py:23
  118.5 1.5 multiply_subtract_fusion
  120.1 9.7 %all_gather.12 = f32[32,2048]{1,0:T(8,128)S(1)} all-gather(f32[32,512]{1,0:T(8,128)S(1)} %get-tuple-element.14), channel_id=1, replica_groups=mesh['replica'=4,'fsdp'=64] {'replica'}, dimensions={1}, use_global_device_ids=true | all-gather | bytes 327680 | tf_op jit(solution)/shard_map/all_gather | solution.py:33
  129.8 0.7 pad_maximum_fusion
  130.5 0.0 all-gather.2.cloned.1.call-update
  130.5 365.9 %all-gather.2.cloned.1.call-done = bf16[2048,3072]{1,0:T(8,128)(2,1)} async-done(((bf16[32,3072]{1,0:T(8,128)(2,1)}), bf16[2048,3072]{1,0:T(8,128)(2,1)}) %all-gather.2.cloned.1.call-update) | async-done | bytes 12582928 | tf_op jit(solution)/shard_map/all_gather | solution.py:35
  496.4 0.0 copy-done
  496.4 8.3 %fusion = bf16[256,3072]{0,1:T(8,128)(2,1)S(1)} fusion(bf16[2048,3072]{1,0:T(8,128)(2,1)} %all-gather.2.cloned.1.call-done, bf16[256,2048]{1,0:T(8,128)(2,1)S(1)} %copy-done), kind=kOutput, calls=%fused_computation.1 | convolution fusion | flops 3222011904 | bytes 15204352 | tf_op jit(solution)/shard_map/dot_general | solution.py:36
  504.7 1.7 copy.17
  506.5 0.7 copy.21
  507.2 0.6 copy.22
  507.8 0.6 copy.23
  (3 shorter events, 0.0 us)
Async XLA Ops:
  7.2 489.2 %copy-start = (bf16[256,2048]{1,0:T(8,128)(2,1)S(1)}, bf16[256,2048]{1,0:T(8,128)(2,1)}, u32[]{:S(2)}) copy-start(bf16[256,2048]{1,0:T(8,128)(2,1)} %param.10) | copy-start | bytes 3145732
  7.2 41.2 %reduce-scatter.6.cloned.1.call-start = ((), (), s32[]{:S(2)}) async-start(), calls=%async_computation.4 | async-start | bytes 81920 | tf_op jit(solution)/shard_map/reduce_scatter | solution.py:23
  8.8 73.7 %reduce-scatter.8.cloned.1.call-start = ((), (), s32[]{:S(2)}) async-start(), calls=%async_computation.5 | async-start | bytes 81920 | tf_op jit(solution)/shard_map/reduce_scatter | solution.py:23
  10.4 108.2 %reduce-scatter.4.cloned.1.call-start = ((), (), s32[]{:S(2)}) async-start(), calls=%async_computation.3 | async-start | bytes 327680 | tf_op jit(solution)/shard_map/reduce_scatter | solution.py:23
  12.2 484.3 %all-gather.2.cloned.1.call-start = ((), (), s32[]{:S(2)}) async-start(), calls=%async_computation.6 | async-start | bytes 12779520 | tf_op jit(solution)/shard_map/all_gather | solution.py:35
Sparse Core Ops, SparseCore 0:
  11.2 37.1 reduce-scatter.5
  51.6 30.8 reduce-scatter.7
  85.8 32.7 reduce-scatter.3
  130.6 365.7 all-gather.1
where the time goes:
time: 515 us
  waiting for transfers between devices  451 us (88%)
  blocking collectives  27.9 us (5%)
  between operations  13.8 us (3%)
  other arithmetic  9.75 us (2%)
  matrix products  8.3 us (2%)
    all_gather x1, waiting for transfers between devices, per_device(): fresh = lax.all_gather(local_fresh, 'fsdp', axis=0, tiled=True)  366 us
    reduce_scatter x3, waiting for transfers between devices, per_device(): lax.psum_scatter(differences, 'replica', scatter_dimension=1, tiled=True)  85.3 us
    all_gather x3, blocking collectives, per_device(): lax.all_gather(tuple(owned_outer), 'replica', axis=1, tiled=True)  27.9 us
  transfers between devices with their start and end apart: 4, of which 4 were waited for; matrix products, arithmetic and copies ran while one was open for 1% of the time, Pallas kernels for 0%

commit v1 on v0

--- a/solution.py
+++ b/solution.py
@@ -32,7 +32,9 @@
         owned_moment.append(new_moment)
     full_outer = lax.all_gather(tuple(owned_outer), "replica", axis=1, tiled=True)
     local_fresh = jnp.concatenate([weight.astype(jnp.bfloat16) for weight in full_outer], axis=1)
-    fresh = lax.all_gather(local_fresh, "fsdp", axis=0, tiled=True)
+    fresh = jnp.concatenate(
+        lax.all_to_all(jnp.stack([local_fresh] * lax.axis_size("fsdp")), "fsdp", 0, 0), axis=0
+    )
     projected = jnp.dot(tokens, fresh, preferred_element_type=jnp.float32).astype(jnp.bfloat16)
     return (
         projected,

time: 515 us -> 434 us (0.84)
  waiting for transfers between devices: 451 us -> 85.4 us
  blocking collectives: 27.9 us -> 311 us
  local copies, waits for them, and re-layouts: 3.71 us -> 9.85 us
    all_gather x1 -> x0, waiting for transfers between devices: 366 us -> none  [per_device(): fresh = lax.all_gather(local_fresh, 'fsdp', axis=0, tiled=True)]
    all_to_all x0 -> x1, blocking collectives: none -> 283 us  [per_device(): lax.all_to_all(jnp.stack([local_fresh] * lax.axis_size('fsdp')), 'fsdp',...]
    another operation x0 -> x1, local copies, waits for them, and re-layouts: none -> 6.14 us  [per_device(): jnp.stack([local_fresh] * lax.axis_size('fsdp'))]
  transfers between devices with their start and end apart: 4 -> 3, of which waited for: 4 -> 3; matrix products, arithmetic and copies ran while one was open for 1% -> 1% of each run, Pallas kernels for 0% -> 0%
where the time goes in v1:
time: 434 us
  blocking collectives  311 us (72%)
  waiting for transfers between devices  85.4 us (20%)
  between operations  13.8 us (3%)
  local copies, waits for them, and re-layouts  9.85 us (2%)
  other arithmetic  9.07 us (2%)
    all_to_all x1, blocking collectives, per_device(): lax.all_to_all(jnp.stack([local_fresh] * lax.axis_size('fsdp')), 'fsdp',...  283 us
    reduce_scatter x3, waiting for transfers between devices, per_device(): lax.psum_scatter(differences, 'replica', scatter_dimension=1, tiled=True)  85.4 us
    all_gather x3, blocking collectives, per_device(): lax.all_gather(tuple(owned_outer), 'replica', axis=1, tiled=True)  27.9 us
  transfers between devices with their start and end apart: 3, of which 3 were waited for; matrix products, arithmetic and copies ran while one was open for 1% of the time, Pallas kernels for 0%

profile of v1, /device:TPU:16, one launch (start us, length us, event | category | flops | bytes accessed | tf_op | source)
XLA Modules:
  0.0 433.5 jit_solution(16940068154737034783)
XLA Ops:
  7.2 0.0 copy-start
  7.2 0.0 reduce-scatter.6.cloned.1.call-start
  7.2 1.6 convert_subtract_fusion.2
  8.8 0.0 reduce-scatter.6.cloned.1.call-update
  8.8 0.0 reduce-scatter.8.cloned.1.call-start
  8.9 1.5 convert_subtract_fusion.1
  10.3 0.0 reduce-scatter.8.cloned.1.call-update
  10.4 0.0 reduce-scatter.4.cloned.1.call-start
  10.4 1.7 convert_subtract_fusion
  12.1 0.0 reduce-scatter.4.cloned.1.call-update
  12.2 36.2 %reduce-scatter.6.cloned.1.call-done = f32[32,128]{1,0:T(8,128)} async-done(((f32[32,512]{1,0:T(8,128)}), f32[32,128]{1,0:T(8,128)}) %reduce-scatter.6.cloned.1.call-update) | async-done | bytes 16400 | tf_op jit(solution)/shard_map/reduce_scatter | solution.py:23
  48.4 1.4 multiply_subtract_fusion.2
  49.8 9.1 %all_gather.10 = f32[32,512]{1,0:T(8,128)S(1)} all-gather(f32[32,128]{1,0:T(8,128)S(1)} %get-tuple-element.16), channel_id=1, replica_groups=mesh['replica'=4,'fsdp'=64] {'replica'}, dimensions={1}, use_global_device_ids=true | all-gather | bytes 81920 | tf_op jit(solution)/shard_map/all_gather | solution.py:33
  58.9 23.6 %reduce-scatter.8.cloned.1.call-done = f32[32,128]{1,0:T(8,128)} async-done(((f32[32,512]{1,0:T(8,128)}), f32[32,128]{1,0:T(8,128)}) %reduce-scatter.8.cloned.1.call-update) | async-done | bytes 16400 | tf_op jit(solution)/shard_map/reduce_scatter | solution.py:23
  82.5 1.4 multiply_subtract_fusion.1
  83.9 9.1 %all_gather.11 = f32[32,512]{1,0:T(8,128)S(1)} all-gather(f32[32,128]{1,0:T(8,128)S(1)} %get-tuple-element.18), channel_id=1, replica_groups=mesh['replica'=4,'fsdp'=64] {'replica'}, dimensions={1}, use_global_device_ids=true | all-gather | bytes 81920 | tf_op jit(solution)/shard_map/all_gather | solution.py:33
  93.0 25.5 %reduce-scatter.4.cloned.1.call-done = f32[32,512]{1,0:T(8,128)} async-done(((f32[32,2048]{1,0:T(8,128)}), f32[32,512]{1,0:T(8,128)}) %reduce-scatter.4.cloned.1.call-update) | async-done | bytes 65552 | tf_op jit(solution)/shard_map/reduce_scatter | solution.py:23
  118.5 1.5 multiply_subtract_fusion
  120.1 9.7 %all_gather.9 = f32[32,2048]{1,0:T(8,128)S(1)} all-gather(f32[32,512]{1,0:T(8,128)S(1)} %get-tuple-element.14), channel_id=1, replica_groups=mesh['replica'=4,'fsdp'=64] {'replica'}, dimensions={1}, use_global_device_ids=true | all-gather | bytes 327680 | tf_op jit(solution)/shard_map/all_gather | solution.py:33
  129.8 6.1 %stack.2 = bf16[64,32,3072]{2,1,0:T(8,128)(2,1)} broadcast(bf16[32,3072]{1,0:T(8,128)(2,1)S(1)} %pad_maximum_fusion), dimensions={1,2} | broadcast | bytes 12779520 | tf_op jit(solution)/shard_map/stack | solution.py:36
  136.0 283.3 %all_to_all.5 = bf16[64,32,3072]{2,1,0:T(8,128)(2,1)S(1)} all-to-all(bf16[64,32,3072]{2,1,0:T(8,128)(2,1)} %stack.2), channel_id=1, replica_groups=mesh['replica'=4,'fsdp'=64] {'fsdp'}, dimensions={0} | all-to-all | bytes 25165824 | tf_op jit(solution)/shard_map/all_to_all | solution.py:36
  419.3 0.0 copy-done
  419.3 4.0 fusion
  423.3 1.7 copy.17
  425.1 0.7 copy.21
  425.8 0.6 copy.22
  426.4 0.6 copy.23
  (4 shorter events, 0.0 us)
Async XLA Ops:
  7.2 412.1 %copy-start = (bf16[256,2048]{1,0:T(8,128)(2,1)S(1)}, bf16[256,2048]{1,0:T(8,128)(2,1)}, u32[]{:S(2)}) copy-start(bf16[256,2048]{1,0:T(8,128)(2,1)} %param.10) | copy-start | bytes 3145732
  7.2 41.2 %reduce-scatter.6.cloned.1.call-start = ((), (), s32[]{:S(2)}) async-start(), calls=%async_computation.5 | async-start | bytes 81920 | tf_op jit(solution)/shard_map/reduce_scatter | solution.py:23
  8.8 73.7 %reduce-scatter.8.cloned.1.call-start = ((), (), s32[]{:S(2)}) async-start(), calls=%async_computation.6 | async-start | bytes 81920 | tf_op jit(solution)/shard_map/reduce_scatter | solution.py:23
  10.4 108.2 %reduce-scatter.4.cloned.1.call-start = ((), (), s32[]{:S(2)}) async-start(), calls=%async_computation.4 | async-start | bytes 327680 | tf_op jit(solution)/shard_map/reduce_scatter | solution.py:23
Sparse Core Ops, SparseCore 0:
  11.2 37.1 reduce-scatter.5
  51.6 30.8 reduce-scatter.7
  85.8 32.7 reduce-scatter.3
